TPU v7x, 512 devices: a whole 4x4x16 slice. The times are simulated.
512 devices in a mesh: dp: 512 (over z, x, y, core).
Axes of the slice: x: 4, y: 4, z: 16, core: 2. Of those that a mesh axis runs over, the one named last changes fastest.
Arguments:
- inputs: bfloat16 [2048, 199, 512], P('dp'), may hold values from -6 to 6
- weights: bfloat16 [2, 262144], replicated, may hold values from -0.1875 to 0.1875
- ln_gain: float32 [512], replicated, may hold values from 0.45 to 2.16
- ln_bias: float32 [512], replicated, may hold values from -3 to 3
- projection: bfloat16 [512, 1024], replicated, may hold values from -0.25 to 0.25
- targets: float32 [2048, 1024], P('dp'), may hold values from -6 to 6
- master: float32 [2, 262144], P(None, 'dp'), may hold values from -0.006 to 0.006
- first_moment: float32 [2, 262144], P(None, 'dp'), may hold values from -0.0006 to 0.0006
- second_moment: float32 [2, 262144], P(None, 'dp'), may hold values from 1e-11 to 1e-08
Outputs:
- input_grad: bfloat16 [2048, 199, 512], P('dp')
- update: float32 [2, 262144], P(None, 'dp')
- new_master: float32 [2, 262144], P(None, 'dp')
- new_first: float32 [2, 262144], P(None, 'dp')
- new_second: float32 [2, 262144], P(None, 'dp')
- new_weights: bfloat16 [2, 262144], replicated
All inputs are finite; a program needn't handle non-finite values.
Results may differ from a plain program's by a relative error of at most 0.006.
Values may be sent and summed in bfloat16 or wider, within the bound.
No kernel may reach another device: no remote copies, remote signals or barrier semaphores. Data moves between devices by JAX's collectives and lax.ppermute only.
A program may use at most 64 MiB of HBM per device.

v0:
```python
import jax
import jax.numpy as jnp
from jax import lax
from jax.sharding import PartitionSpec as P


def norm_act(pre, gain, bias):
    center = pre - jnp.mean(pre, axis=-1, keepdims=True)
    spread = jnp.mean(center * center, axis=-1, keepdims=True)
    normed = center * lax.rsqrt(spread + 1e-05)
    return jax.nn.gelu(normed * gain + bias, approximate=False)


def local_pass(inputs, weights, ln_gain, ln_bias, projection, targets):
    clips, frames_in, chans = inputs.shape
    taps = weights.shape[0]
    frames_out = (frames_in - taps) // taps + 1
    windows = inputs[:, : frames_out * taps].reshape(clips, frames_out, taps, chans)
    kernel = weights.reshape(taps, chans, chans)
    pre = jnp.einsum("bfki,koi->bfo", windows, kernel, preferred_element_type=jnp.float32)
    act, pull = jax.vjp(lambda value: norm_act(value, ln_gain, ln_bias), pre)
    pooled = jnp.mean(act, axis=1).astype(jnp.bfloat16)
    predicted = jnp.dot(pooled, projection, preferred_element_type=jnp.float32)
    miss = (predicted - targets).astype(jnp.bfloat16)
    back = lax.dot_general(
        miss, projection, (((1,), (1,)), ((), ())), preferred_element_type=jnp.float32
    )
    upstream = jnp.broadcast_to(back[:, None, :] / frames_out, act.shape)
    dpre = pull(upstream)[0].astype(jnp.bfloat16)
    dwin = jnp.einsum("bfo,koi->bfki", dpre, kernel, preferred_element_type=jnp.float32).astype(
        jnp.bfloat16
    )
    dinput = dwin.reshape(clips, frames_out * taps, chans)
    tail = jnp.zeros((clips, frames_in - frames_out * taps, chans), jnp.bfloat16)
    return (windows, dpre, jnp.concatenate([dinput, tail], axis=1))


def body(
    inputs, weights, ln_gain, ln_bias, projection, targets, master, first_moment, second_moment
):
    windows, dpre, input_grad = local_pass(inputs, weights, ln_gain, ln_bias, projection, targets)
    taps = weights.shape[0]
    term = jnp.einsum("bfo,bfki->koi", dpre, windows, preferred_element_type=jnp.float32)
    grad = lax.psum_scatter(term.reshape(taps, -1), "dp", scatter_dimension=1, tiled=True)
    squares = lax.psum(jnp.sum(grad * grad), "dp")
    scale = jnp.minimum(1.0, 1.0 / (jnp.sqrt(squares) + 1e-06))
    clipped = scale * grad
    new_first = 0.9 * first_moment + 0.1 * clipped
    new_second = 0.999 * second_moment + 0.001 * clipped * clipped
    update = new_first / (1.0 - 0.9**20) / (jnp.sqrt(new_second / (1.0 - 0.999**20)) + 1e-08)
    new_master = master - 0.0001 * (update + 0.01 * master)
    new_weights = lax.all_gather(new_master.astype(jnp.bfloat16), "dp", axis=1, tiled=True)
    return (input_grad, update, new_master, new_first, new_second, new_weights)


def solution(mesh):
    return jax.shard_map(
        body,
        mesh=mesh,
        in_specs=(
            P("dp", None, None),
            P(),
            P(),
            P(),
            P(),
            P("dp", None),
            P(None, "dp"),
            P(None, "dp"),
            P(None, "dp"),
        ),
        out_specs=(
            P("dp", None, None),
            P(None, "dp"),
            P(None, "dp"),
            P(None, "dp"),
            P(None, "dp"),
            P(),
        ),
        check_vma=False,
    )
```

profile of v0, /device:TPU:1, one launch (start us, length us, event | category | flops | bytes accessed | tf_op | source)
XLA Modules:
  0.0 786.2 jit_solution(7399412350724682430)
XLA Ops:
  7.2 0.0 copy-start
  7.2 0.0 all-reduce.4.cloned.1.call-start
  7.2 1.5 slice.3
  8.7 0.0 copy-start.1
  8.7 0.0 copy-start.5
  8.8 0.0 copy-start.6
  8.8 2.3 fusion.26
  11.1 0.0 copy-start.7
  11.1 0.3 multiply_reduce_fusion.2
  11.3 0.0 copy-done.1
  11.4 0.0 copy-done.5
  11.4 0.0 copy-done.6
  11.4 2.2 multiply_reduce_fusion.1
  13.6 0.0 copy-done
  13.6 0.0 copy-done.7
  13.6 0.5 broadcast_multiply_fusion
  14.1 0.0 copy-start.2
  14.1 0.7 multiply_reduce_fusion
  14.9 0.8 fusion.24
  15.7 0.0 copy-start.3
  15.8 0.9 copy-done.3
  16.6 0.0 copy-done.2
  16.6 0.9 convolution_bitcast_fusion
  17.5 2.9 copy.28
  20.5 0.0 copy-start.8
  20.5 0.0 copy-start.9
  20.5 0.0 copy-start.10
  20.5 0.0 copy-start.4
  20.5 0.0 copy-start.11
  20.5 0.0 all-reduce.4.cloned.1.call-update
  20.5 0.0 all-gather.2.cloned.1.call-start
  20.6 487.3 %all-reduce.4.cloned.1.call-done = f32[2,262144]{1,0:T(2,128)} async-done(((f32[2,262144]{1,0:T(2,128)}), f32[2,262144]{1,0:T(2,128)}) %all-reduce.4.cloned.1.call-update) | async-done | bytes 2097168
  507.8 1.3 multiply_reduce_fusion.3
  509.1 103.3 %psum.7 = f32[]{:T(128)} all-reduce(f32[]{:T(128)} %multiply_reduce_fusion.3), channel_id=1, replica_groups=mesh['dp'=512] {'dp'}, use_global_device_ids=true, to_apply=%region_7.0 | all-reduce | flops 1 | bytes 8 | tf_op jit(solution)/shard_map/psum | solution.py:45
  613.2 0.0 copy-done.8
  613.2 0.0 copy-done.9
  613.2 0.0 copy-done.10
  613.2 1.3 fusion.22
  614.5 0.0 all-gather.2.cloned.1.call-update
  614.5 0.0 copy-done.4
  614.5 0.0 copy-done.11
  614.6 0.7 convolution_convert_fusion
  615.2 0.6 copy.20
  615.9 1.2 concatenate.3
  617.1 159.7 %all-gather.2.cloned.1.call-done = bf16[2,262144]{1,0:T(2,128)(2,1)} async-done(((bf16[2,512]{1,0:T(2,128)(2,1)}), bf16[2,262144]{1,0:T(2,128)(2,1)}) %all-gather.2.cloned.1.call-update) | async-done | bytes 1048592 | tf_op jit(solution)/shard_map/all_gather | solution.py:52
  776.8 2.6 copy.47
  (4 shorter events, 0.0 us)
Async XLA Ops:
  7.2 6.5 copy-start
  7.2 500.6 %all-reduce.4.cloned.1.call-start = ((), (), s32[]{:S(2)}) async-start(), calls=%async_computation.1 | async-start | bytes 4194304
  8.7 2.6 copy-start.1
  8.7 2.6 copy-start.5
  8.8 2.6 copy-start.6
  11.1 2.6 copy-start.7
  14.1 2.5 copy-start.2
  15.7 0.9 copy-start.3
  20.5 592.7 %copy-start.8 = (f32[2,512]{1,0:T(2,128)S(1)}, f32[2,512]{1,0:T(2,128)}, u32[]{:S(2)}) copy-start(f32[2,512]{1,0:T(2,128)} %param.15) | copy-start | bytes 12292
  20.5 592.7 %copy-start.9 = (f32[2,512]{1,0:T(2,128)S(1)}, f32[2,512]{1,0:T(2,128)}, u32[]{:S(2)}) copy-start(f32[2,512]{1,0:T(2,128)} %param.16) | copy-start | bytes 12292
  20.5 592.7 %copy-start.10 = (f32[2,512]{1,0:T(2,128)S(1)}, f32[2,512]{1,0:T(2,128)}, u32[]{:S(2)}) copy-start(f32[2,512]{1,0:T(2,128)} %param.17) | copy-start | bytes 12292
  20.5 594.1 %copy-start.4 = (f32[4,99,512]{2,1,0:T(8,128)S(1)}, f32[4,99,512]{2,1,0:T(8,128)}, u32[]{:S(2)}) copy-start(f32[4,99,512]{2,1,0:T(8,128)} %copy-done.3) | copy-start | bytes 2433028
  20.5 594.1 %copy-start.11 = (bf16[2,262144]{1,0:T(2,128)(2,1)S(1)}, bf16[2,262144]{1,0:T(2,128)(2,1)}, u32[]{:S(2)}) copy-start(bf16[2,262144]{1,0:T(2,128)(2,1)} %param.10) | copy-start | bytes 3145732
  20.5 756.3 %all-gather.2.cloned.1.call-start = ((), (), s32[]{:S(2)}) async-start(), calls=%async_computation | async-start | bytes 1050624 | tf_op jit(solution)/shard_map/all_gather | solution.py:52
Sparse Core Ops, SparseCore 0:
  20.6 487.1 all-reduce.3
  614.7 162.0 all-gather.1
where the time goes:
time: 787 us; the launch traced here: 786 us
  waiting for transfers between devices  647 us (82%)
  blocking collectives  103 us (13%)
  between operations  15 us (2%)
  local copies, waits for them, and re-layouts  9.76 us (1%)
    unnamed x3, waiting for transfers between devices  487 us
    all_gather x1, waiting for transfers between devices, body(): lax.all_gather(new_master.astype(jnp.bfloat16), 'dp', axis=1, tiled=True)  160 us
    psum x1, blocking collectives, body(): squares = lax.psum(jnp.sum(grad * grad), 'dp')  103 us
  transfers between devices with their start and end apart: 2, of which 2 were waited for; matrix products, arithmetic and copies ran while one was open for 0% of the time, Pallas kernels for 0%

commit v1 on v0

--- a/solution.py
+++ b/solution.py
@@ -49,7 +49,9 @@
     new_second = 0.999 * second_moment + 0.001 * clipped * clipped
     update = new_first / (1.0 - 0.9**20) / (jnp.sqrt(new_second / (1.0 - 0.999**20)) + 1e-08)
     new_master = master - 0.0001 * (update + 0.01 * master)
-    new_weights = lax.all_gather(new_master.astype(jnp.bfloat16), "dp", axis=1, tiled=True)
+    part = new_master.astype(jnp.bfloat16)
+    repeated = jnp.stack([part] * lax.axis_size("dp"))
+    new_weights = jnp.concatenate(lax.all_to_all(repeated, "dp", 0, 0), axis=1)
     return (input_grad, update, new_master, new_first, new_second, new_weights)
 
 

time: 787 us -> 695 us (0.88)
  waiting for transfers between devices: 647 us -> 542 us
  starting transfers between devices: 0.08 us -> 12.5 us
    all_gather x1 -> x0, waiting for transfers between devices: 160 us -> none  [body(): lax.all_gather(new_master.astype(jnp.bfloat16), 'dp', axis=1, tiled=True)]
    all_to_all x0 -> x1, waiting for transfers between devices: none -> 54.4 us  [body(): new_weights = jnp.concatenate(lax.all_to_all(repeated, 'dp', 0, 0), axis=1)]
    all_to_all x0 -> x1, starting transfers between devices: none -> 12.5 us  [body(): new_weights = jnp.concatenate(lax.all_to_all(repeated, 'dp', 0, 0), axis=1)]
    unnamed x3 -> x2, waiting for transfers between devices: 487 us -> 487 us
  transfers between devices with their start and end apart: 2 -> 2, of which waited for: 2 -> 2; matrix products, arithmetic and copies ran while one was open for 0% -> 1% of each run, Pallas kernels for 0% -> 0%
where the time goes in v1:
time: 695 us; the launch traced here: 694 us
  waiting for transfers between devices  542 us (78%)
  blocking collectives  103 us (15%)
  between operations  15 us (2%)
  starting transfers between devices  12.5 us (2%)
  local copies, waits for them, and re-layouts  9.67 us (1%)
    unnamed x2, waiting for transfers between devices  487 us
    psum x1, blocking collectives, body(): squares = lax.psum(jnp.sum(grad * grad), 'dp')  103 us
    all_to_all x1, waiting for transfers between devices, body(): new_weights = jnp.concatenate(lax.all_to_all(repeated, 'dp', 0, 0), axis=1)  54.4 us
  transfers between devices with their start and end apart: 2, of which 2 were waited for; matrix products, arithmetic and copies ran while one was open for 1% of the time, Pallas kernels for 0%

profile of v1, /device:TPU:1, one launch (start us, length us, event | category | flops | bytes accessed | tf_op | source)
XLA Modules:
  0.0 694.4 jit_solution(4244503967939782309)
XLA Ops:
  7.2 0.0 copy-start
  7.2 0.0 all-reduce.4.cloned.1.call-start
  7.2 1.5 slice.3
  8.7 0.0 copy-start.1
  8.7 0.0 copy-start.5
  8.8 0.0 copy-start.6
  8.8 2.3 fusion.26
  11.1 0.0 copy-start.7
  11.1 0.3 multiply_reduce_fusion.2
  11.3 0.0 copy-done.1
  11.4 0.0 copy-done.5
  11.4 0.0 copy-done.6
  11.4 2.2 multiply_reduce_fusion.1
  13.6 0.0 copy-done
  13.6 0.0 copy-done.7
  13.6 0.5 broadcast_multiply_fusion
  14.1 0.0 copy-start.2
  14.1 0.7 multiply_reduce_fusion
  14.9 0.8 fusion.24
  15.7 0.0 copy-start.3
  15.8 0.9 copy-done.3
  16.6 0.0 copy-done.2
  16.6 0.9 convolution_bitcast_fusion
  17.5 2.9 copy.28
  20.4 0.0 copy-start.8
  20.5 0.0 copy-start.9
  20.5 0.0 copy-start.10
  20.5 0.0 all-reduce.4.cloned.1.call-update
  20.5 0.0 copy-start.4
  20.5 487.3 %all-reduce.4.cloned.1.call-done = f32[2,262144]{1,0:T(2,128)} async-done(((f32[2,262144]{1,0:T(2,128)}), f32[2,262144]{1,0:T(2,128)}) %all-reduce.4.cloned.1.call-update) | async-done | bytes 2097168
  507.8 1.3 multiply_reduce_fusion.3
  509.1 103.3 %psum.7 = f32[]{:T(128)} all-reduce(f32[]{:T(128)} %multiply_reduce_fusion.3), channel_id=1, replica_groups=mesh['dp'=512] {'dp'}, use_global_device_ids=true, to_apply=%region_7.0 | all-reduce | flops 1 | bytes 8 | tf_op jit(solution)/shard_map/psum | solution.py:45
  613.1 0.0 copy-done.8
  613.2 0.0 copy-done.9
  613.2 0.0 copy-done.10
  613.2 1.3 fusion.22
  614.5 1.5 stack.2
  616.0 12.5 %all-to-all-start = ((bf16[512,2,512]{2,1,0:T(2,128)(2,1)}), bf16[512,2,512]{2,1,0:T(2,128)(2,1)S(1)}, u32[]{:S(2)}, u32[]{:S(2)}) async-start(bf16[512,2,512]{2,1,0:T(2,128)(2,1)} %stack.2), calls=%async_computation | async-start | bytes 2097152 | tf_op jit(solution)/shard_map/all_to_all | solution.py:54
  628.5 0.0 copy-done.4
  628.5 1.9 convolution_convert_fusion
  630.4 0.6 copy.20
  631.0 1.2 concatenate.3
  632.2 54.4 %all-to-all-done = bf16[512,2,512]{2,1,0:T(2,128)(2,1)S(1)} async-done(((bf16[512,2,512]{2,1,0:T(2,128)(2,1)}), bf16[512,2,512]{2,1,0:T(2,128)(2,1)S(1)}, u32[]{:S(2)}, u32[]{:S(2)}) %all-to-all-start) | async-done | bytes 1048608 | tf_op jit(solution)/shard_map/all_to_all | solution.py:54
  686.6 1.0 copy.47
  (4 shorter events, 0.0 us)
Async XLA Ops:
  7.2 6.5 copy-start
  7.2 500.6 %all-reduce.4.cloned.1.call-start = ((), (), s32[]{:S(2)}) async-start(), calls=%async_computation.1 | async-start | bytes 4194304
  8.7 2.6 copy-start.1
  8.7 2.6 copy-start.5
  8.8 2.6 copy-start.6
  11.1 2.6 copy-start.7
  14.1 2.5 copy-start.2
  15.7 0.9 copy-start.3
  20.4 592.7 %copy-start.8 = (f32[2,512]{1,0:T(2,128)S(1)}, f32[2,512]{1,0:T(2,128)}, u32[]{:S(2)}) copy-start(f32[2,512]{1,0:T(2,128)} %param.15) | copy-start | bytes 12292
  20.5 592.7 %copy-start.9 = (f32[2,512]{1,0:T(2,128)S(1)}, f32[2,512]{1,0:T(2,128)}, u32[]{:S(2)}) copy-start(f32[2,512]{1,0:T(2,128)} %param.16) | copy-start | bytes 12292
  20.5 592.7 %copy-start.10 = (f32[2,512]{1,0:T(2,128)S(1)}, f32[2,512]{1,0:T(2,128)}, u32[]{:S(2)}) copy-start(f32[2,512]{1,0:T(2,128)} %param.17) | copy-start | bytes 12292
  20.5 608.0 %copy-start.4 = (f32[4,99,512]{2,1,0:T(8,128)S(1)}, f32[4,99,512]{2,1,0:T(8,128)}, u32[]{:S(2)}) copy-start(f32[4,99,512]{2,1,0:T(8,128)} %copy-done.3) | copy-start | bytes 2433028
  616.0 70.6 %all-to-all-start = ((bf16[512,2,512]{2,1,0:T(2,128)(2,1)}), bf16[512,2,512]{2,1,0:T(2,128)(2,1)S(1)}, u32[]{:S(2)}, u32[]{:S(2)}) async-start(bf16[512,2,512]{2,1,0:T(2,128)(2,1)} %stack.2), calls=%async_computation | async-start | bytes 2097152 | tf_op jit(solution)/shard_map/all_to_all | solution.py:54
Sparse Core Ops, SparseCore 0:
  20.6 487.1 all-reduce.3
